TPU v7x, 32 devices: a whole 2x2x4 slice. The times are simulated.
32 devices in a mesh: dom: 8 (over z, x), sub: 4 (over y, core).
Axes of the slice: x: 2, y: 2, z: 4, core: 2. Of those that a mesh axis runs over, the one named last changes fastest.
Arguments:
- positions: float32 [3, 1048576], P(None, ('dom', 'sub')), may hold values from -0.11 to 1.11
- velocities: float32 [3, 1048576], P(None, ('dom', 'sub')), may hold values from -3 to 3
- masses: float32 [1048576], P(('dom', 'sub')), may hold values from 0.003 to 0.012
- accel_prev: float32 [3, 1048576], P(None, ('dom', 'sub')), may hold values from -180 to 180
- active: int32 [1048576], P(('dom', 'sub')), may hold values from 0 to 1, as said below
- bucket_top: int32 [4096], P(('dom', 'sub')), may hold values from 0 to 4095
- near_list: int32 [4096, 4], P(('dom', 'sub')), may hold values from 0 to 511, as said below
- cell_list: int32 [4096, 64], P(('dom', 'sub')), may hold values from 0 to 1023
- top_list: int32 [4096, 32], P(('dom', 'sub')), may hold values from 0 to 4095
- essential: int32 [8, 4, 8, 32], P('dom', 'sub'), may hold values from 0 to 511
- work: int32 [1280], P(('dom', 'sub')), may hold values from 0 to 511, as said below
Outputs:
- vel_out: float32 [3, 1048576], P(None, ('dom', 'sub'))
- pos_out: float32 [3, 1048576], P(None, ('dom', 'sub'))
Inputs may be any that keep to these rules, and one draw needn't show every extreme that they name: near_list[n, 0] is the group-local number of bucket n itself; every entry of row n names a bucket of n's group whose top cell differs from n's by at most one in each of the three top-cell coordinates. A bucket holds an active particle exactly when its group-local number appears in its group's block of work. `work`: entries g * 4 * 40 to (g + 1) * 4 * 40 - 1 are the block of domain group g and name distinct group-local buckets; in every group one device holds 128 of the named buckets.
All inputs are finite; a program needn't handle non-finite values.
Results may differ from a plain program's by a relative error of at most 0.0003.
Values sent between devices are 32-bit elements; how exact they have to be, the bound alone decides.
No kernel may reach another device: no remote copies, remote signals or barrier semaphores. Data moves between devices by JAX's collectives and lax.ppermute only.
A program may use at most 64 MiB of HBM per device.

v0:
```python
import functools

import jax
import jax.numpy as jnp
from jax import lax
from jax.experimental import pallas as pl
from jax.experimental.pallas import tpu as pltpu
from jax.sharding import PartitionSpec as P


TOP_SIDE = 16
TOP = TOP_SIDE**3
DT = 0.01
EPS = 0.0025
MASS_FLOOR = 0.5
LANES = 128
ROWS = 16
SENT = 11
LOWER = 256
PARTS = 4 * ROWS
CHUNKS = 1
CELL_CHUNK = 32
CELL_SPAN = 4


f32 = jnp.float32
bf16 = jnp.bfloat16


def other_slot(index, size, me):
    if size & (size - 1) == 0:
        return index ^ (me * size)
    return ((index // size) ^ me) * size + index % size


def to_tiles(three, one):
    flat = jnp.concatenate([three, one[None]], axis=0)
    count = flat.shape[1] // (2 * LANES)
    return flat.reshape(4, count, 2, LANES).transpose(1, 2, 0, 3).reshape(count, 8, LANES)


def from_tiles(tiles):
    count = tiles.shape[0]
    flat = tiles.reshape(count, 2, 4, LANES).transpose(2, 0, 1, 3).reshape(4, count * 2 * LANES)
    return flat[:3]


def sub_gather(block, sub_count, before_pass=None):
    parts = [None] * sub_count
    parts[0] = block
    for step in range(0, sub_count, 2):
        if step:
            parts[step] = lax.ppermute(block, "sub", [(i, i ^ step) for i in range(sub_count)])
            if before_pass is not None:
                parts[step], _ = lax.optimization_barrier((parts[step], before_pass))
    for step in range(0, sub_count, 2):
        parts[step + 1] = lax.ppermute(parts[step], "sub", [(i, i ^ 1) for i in range(sub_count)])
    return parts


def row_iota(shape=(8, LANES)):
    return lax.broadcasted_iota(jnp.int32, shape, 0)


def rounded(values):
    return values.astype(bf16).astype(f32)


def moments_of(get):
    weights = [get(0, 3), get(1, 3)]
    places = [[get(half, axis) for axis in range(3)] for half in range(2)]

    def total(one, two):
        return jnp.sum(one + two, axis=1, keepdims=True)

    mass = total(weights[0], weights[1])
    centre = [
        total(weights[0] * places[0][axis], weights[1] * places[1][axis]) / mass
        for axis in range(3)
    ]
    off = [[places[half][axis] - centre[axis] for axis in range(3)] for half in range(2)]
    woff = [[weights[half] * off[half][axis] for axis in range(3)] for half in range(2)]

    def second(a, b):
        return total(woff[0][a] * off[0][b], woff[1][a] * off[1][b])

    xx, yy, zz = second(0, 0), second(1, 1), second(2, 2)
    trace = xx + yy + zz
    return [mass] + centre + [
        3.0 * xx - trace,
        3.0 * yy - trace,
        3.0 * zz - trace,
        3.0 * second(0, 1),
        3.0 * second(0, 2),
        3.0 * second(1, 2),
    ]


def write_moments(columns, tops_row, out_ref, bucket_count):
    lane = lax.broadcasted_iota(jnp.int32, (bucket_count, LANES), 1)
    wide = jnp.zeros((bucket_count, LANES), f32)
    for q, column in enumerate(columns):
        wide = jnp.where(lane == q, column, wide)
    turned = jnp.transpose(wide)
    blocks = bucket_count // LANES
    for block in range(blocks):
        at = slice(block * LANES, (block + 1) * LANES)
        rows = jnp.concatenate([turned[:10, at], tops_row[:, at]], axis=0)
        for copy in range(out_ref.shape[0] // (blocks * SENT)):
            start = (copy * blocks + block) * SENT
            out_ref[start : start + SENT, :] = rows


def tile_rows(ref, row, bucket_count):
    return ref[pl.ds(row, bucket_count, stride=8), :]


def first_moments_kernel(tiles_ref, tops_ref, out_ref):
    bucket_count = tiles_ref.shape[0] // 8
    columns = moments_of(lambda half, row: tile_rows(tiles_ref, 4 * half + row, bucket_count))
    write_moments(columns, tops_ref[...], out_ref, bucket_count)


def spread_own(acc_refs, work_ref, me, own_ref, bucket_count):
    own_ref[...] = jnp.zeros_like(own_ref)
    count = work_ref.shape[1]
    for part, acc_ref in enumerate(acc_refs):

        @pl.loop(0, count, unroll=8 if count % 8 == 0 else 1)
        def _(i):
            bucket = work_ref[part, i] - me * bucket_count
            mine = jnp.logical_and(bucket >= 0, bucket < bucket_count)
            slot = pl.multiple_of(jnp.where(mine, bucket, bucket_count) * 8, 8)
            own_ref[pl.ds(slot, 8), :] = acc_ref[i]


def act_rows(tiles):
    count = tiles.shape[0] // 8
    wide = tiles.reshape(count, 8, LANES)
    row = lax.broadcasted_iota(jnp.int32, wide.shape, 1)
    first = jnp.broadcast_to(wide[:, 3:4, :], wide.shape)
    second = jnp.broadcast_to(wide[:, 7:8, :], wide.shape)
    return row % 4 == 3, jnp.where(row < 4, first, second), wide


def second_moments_kernel(
    sub_count, me_ref, work_ref, ahead_ref, tiles_ref, speeds_ref, tops_ref, *refs
):
    acc_refs, (out_ref, places_ref, base_ref, own_ref) = refs[:sub_count], refs[sub_count:]
    bucket_count = tiles_ref.shape[0] // 8
    spread_own(acc_refs, work_ref, me_ref[0], own_ref, bucket_count)

    @pl.loop(0, bucket_count // 8)
    def _(i):
        at = pl.ds(pl.multiple_of(i * 64, 64), 64)
        last, act, ahead = act_rows(ahead_ref[at, :])
        kick = DT * act * own_ref[at, :].reshape(8, 8, LANES)
        base_ref[at, :] = speeds_ref[at, :] + jnp.where(last, 0.0, kick).reshape(64, LANES)
        moved = ahead + DT * kick
        places = jnp.where(last, tiles_ref[at, :].reshape(8, 8, LANES), moved)
        places_ref[at, :] = places.reshape(64, LANES)

    columns = moments_of(lambda half, row: tile_rows(places_ref, 4 * half + row, bucket_count))
    write_moments(columns, tops_ref[...], out_ref, bucket_count)


def final_kernel(sub_count, me_ref, work_ref, base_ref, *refs):
    acc_refs, (out_ref, full_ref) = refs[:sub_count], refs[sub_count:]
    bucket_count = base_ref.shape[0] // 8
    full_ref[: bucket_count * 8, :] = base_ref[...]
    count = work_ref.shape[1]
    last = row_iota() % 4 == 3
    for part, acc_ref in enumerate(acc_refs):

        @pl.loop(0, count, unroll=8 if count % 8 == 0 else 1)
        def _(i):
            bucket = work_ref[part, i] - me_ref[0] * bucket_count
            mine = jnp.logical_and(bucket >= 0, bucket < bucket_count)
            tile = base_ref[pl.ds(pl.multiple_of(jnp.where(mine, bucket, 0) * 8, 8), 8), :]
            act = jnp.where(last, tile, 0.0)
            act = act + pltpu.roll(act, 7, 0) + pltpu.roll(act, 6, 0) + pltpu.roll(act, 5, 0)
            place = pl.ds(pl.multiple_of(jnp.where(mine, bucket, bucket_count) * 8, 8), 8)
            full_ref[place, :] = tile + (0.5 * DT) * act * acc_ref[i]

    out_ref[...] = full_ref[: bucket_count * 8, :]


def traceless(diag, cross):
    trace = diag[0] + diag[1] + diag[2]
    return [3.0 * d - trace for d in diag] + [3.0 * c for c in cross]


def outer(first, second):
    return (
        [first[a] * second[a] for a in range(3)],
        [first[0] * second[1], first[0] * second[2], first[1] * second[2]],
    )


def in_parts(values):
    high, middle, low = three(values)
    return jnp.concatenate([high, middle, low, jnp.ones_like(values)], axis=0)


def build_rows(cells_ref, rows_ref, raw_ref, sums_ref, tops_ref):
    blocks = cells_ref.shape[0] // SENT
    uppers = TOP // LOWER
    sides = LOWER // LANES
    for block in range(blocks):
        start = block * SENT
        if start + ROWS <= cells_ref.shape[0]:
            turned = cells_ref[start : start + ROWS, :]
        else:
            turned = jnp.concatenate(
                [cells_ref[start : start + SENT, :], jnp.zeros((ROWS - SENT, LANES), f32)], axis=0
            )
        rows_ref[block * LANES : (block + 1) * LANES, :PARTS] = jnp.transpose(in_parts(turned))
    side = TOP_SIDE

    def sent(q):
        return cells_ref[pl.ds(q, blocks, stride=SENT), :]

    top_id = sent(10).astype(jnp.int32)
    index = [top_id // (side * side), top_id // side % side, top_id % side]
    mass = sent(0)
    delta = [sent(1 + a) - (index[a].astype(f32) + 0.5) / side for a in range(3)]
    first = [mass * delta[a] for a in range(3)]
    lifted = traceless(*outer(first, delta))
    raw = [mass] + first + [sent(4 + k) + lifted[k] for k in range(6)]
    for q in range(ROWS):
        raw_ref[q * blocks : (q + 1) * blocks, :] = raw[q] if q < 10 else jnp.zeros_like(mass)
    sums_ref[...] = jnp.zeros_like(sums_ref)
    pair = 2 if blocks % 2 == 0 else 1

    @pl.loop(0, blocks // pair)
    def _(step):
        top, values = [], []
        for part in range(pair):
            block = step * pair + part
            top.append(cells_ref[pl.ds(block * SENT + 10, 1), :])
            values.append(raw_ref[pl.ds(block, ROWS, stride=blocks), :])
        top = jnp.concatenate(top, axis=1).astype(jnp.int32)
        values = jnp.concatenate(values, axis=1)
        high = values.astype(bf16)
        low = (values - high.astype(f32)).astype(bf16)
        width = top.shape[1]
        upper = jnp.broadcast_to(top // LOWER, (ROWS, width))
        lower = jnp.broadcast_to(top % LOWER, (LOWER, width))
        match = lax.broadcasted_iota(jnp.int32, (LOWER, width), 0) == lower
        picks = jnp.where(match, 1.0, 0.0).astype(bf16)
        empty = jnp.zeros_like(high)
        parts = []
        for piece in (high, low):
            left = jnp.concatenate(
                [jnp.where(upper == u, piece, empty) for u in range(uppers)], axis=0
            )
            parts.append(
                lax.dot_general(left, picks, (((1,), (1,)), ((), ())), preferred_element_type=f32)
            )
        both = parts[0] + parts[1]
        for side_at in range(sides):
            rows = slice(side_at * uppers * ROWS, (side_at + 1) * uppers * ROWS)
            sums_ref[rows, :] += both[:, side_at * LANES : (side_at + 1) * LANES]

    cell = lax.broadcasted_iota(jnp.int32, (uppers, LOWER), 0) * LOWER
    cell = cell + lax.broadcasted_iota(jnp.int32, (uppers, LOWER), 1)
    index = [cell // (side * side), cell // side % side, cell % side]

    def summed(q):
        return jnp.concatenate(
            [
                sums_ref[pl.ds(side_at * uppers * ROWS + q, uppers, stride=ROWS), :]
                for side_at in range(sides)
            ],
            axis=1,
        )

    mass = summed(0)
    inverse = 1.0 / jnp.maximum(mass, MASS_FLOOR)
    first = [summed(1 + a) for a in range(3)]
    shift = [first[a] * inverse for a in range(3)]
    lowered = traceless(*outer(first, shift))
    tops = (
        [mass]
        + [(index[a].astype(f32) + 0.5) / side + shift[a] for a in range(3)]
        + [summed(4 + k) - lowered[k] for k in range(6)]
    )
    for q in range(10):
        for side_at in range(sides):
            at = pl.ds(side_at * uppers * ROWS + q, uppers, stride=ROWS)
            tops_ref[at, :] = tops[q][:, side_at * LANES : (side_at + 1) * LANES]
    for u in range(uppers):
        for side_at in range(sides):
            start = blocks * LANES + u * LOWER + side_at * LANES
            rows = (side_at * uppers + u) * ROWS
            rows_ref[start : start + LANES, :PARTS] = jnp.transpose(
                in_parts(tops_ref[rows : rows + ROWS, :])
            )


def cell_terms(off, mass, quad, sums):
    dist = off[0] * off[0] + off[1] * off[1] + off[2] * off[2] + EPS
    inv = lax.rsqrt(dist)
    inv_two = inv * inv
    inv_five = inv_two * inv_two * inv
    along = [
        quad[0] * off[0] + quad[3] * off[1] + quad[4] * off[2],
        quad[3] * off[0] + quad[1] * off[1] + quad[5] * off[2],
        quad[4] * off[0] + quad[5] * off[1] + quad[2] * off[2],
    ]
    both = off[0] * along[0] + off[1] * along[1] + off[2] * along[2]
    radial = mass * dist + 2.5 * both * inv_two
    for a in range(3):
        sums[a] += (along[a] - radial * off[a]) * inv_five


def with_norm(values, extra, scale, last):
    squares = jnp.where(last, 0.0, values * values)
    norm = pltpu.roll(squares, 1, 0) + pltpu.roll(squares, 2, 0) + pltpu.roll(squares, 3, 0)
    return jnp.where(last, norm + extra, scale * values)


def three(values):
    high = rounded(values)
    rest = values - high
    middle = rounded(rest)
    return high, middle, rest - middle


def prepare_near(tile, sources, masses, left_ref, right_ref, pull_ref, target_ref):
    row = row_iota()
    last = row % 4 == 3
    front = row < 4
    mean = jnp.sum(tile, axis=1, keepdims=True)
    mean = jnp.broadcast_to(mean, (8, LANES))
    centre = jnp.where(last, 0.0, (mean + pltpu.roll(mean, 4, 0)) * (0.5 / LANES))
    target = tile - centre
    target_ref[...] = target
    high, middle, low = three(with_norm(target, EPS, -2.0, last))
    plain = jnp.where(last, 1.0, high)
    blocks = [plain, plain, plain, jnp.where(last, high, middle), middle, low]
    turned = [pltpu.roll(block, 4, 0) for block in blocks]
    first = [jnp.where(front, b, t) for b, t in zip(blocks, turned)]
    second = [jnp.where(front, t, b) for b, t in zip(blocks, turned)]
    for half in range(2):
        keep = front if half == 0 else jnp.logical_not(front)
        for side, parts in enumerate((first, second)):
            right_ref[half, :, side * LANES : (side + 1) * LANES] = jnp.concatenate(
                [jnp.where(keep, part, 0.0) for part in parts], axis=0
            ).astype(bf16)
    for k, (source, weights) in enumerate(zip(sources, masses)):
        at = slice(k * LANES, (k + 1) * LANES)
        place = source - centre
        high, middle, low = three(with_norm(place, 0.0, 1.0, last))
        high_one = jnp.where(last, 1.0, high)
        middle_one = jnp.where(last, 1.0, middle)
        stack = jnp.concatenate([high, middle, low, high_one, middle_one, high_one], axis=0)
        left_ref[at, :] = jnp.transpose(stack).astype(bf16)
        mass = jnp.where(last, weights, 0.0)
        mass = mass + pltpu.roll(mass, 7, 0) + pltpu.roll(mass, 6, 0) + pltpu.roll(mass, 5, 0)
        moved = mass * place
        moved_high, mass_high = rounded(moved), rounded(mass)
        pull_ref[:, at] = jnp.concatenate(
            [moved_high, moved - moved_high, mass_high, mass - mass_high], axis=0
        ).astype(bf16)


def near_distances(operand, start, width):
    left_ref, right_ref = operand[:2]
    left = left_ref[start : start + width, :]
    return [jnp.dot(left, right_ref[half], preferred_element_type=f32) for half in range(2)]


def near_pulls(operand, start, width, dist, total):
    pull = operand[2][:, start : start + width]
    weight = [lax.rsqrt((d * d * d).astype(bf16)) for d in dist]
    for half in range(2):
        part = jnp.dot(pull, weight[half], preferred_element_type=f32)
        total[half] = part if total[half] is None else total[half] + part


def near_result(target, total):
    row = row_iota()
    last = row % 4 == 3
    front = row < 4

    def fold(start):
        parts = [t[start : start + 8, :] + t[start + 8 : start + 16, :] for t in total]
        sides = []
        for side in range(2):
            at = slice(side * LANES, (side + 1) * LANES)
            mixed = jnp.where(front, parts[0][:, at], parts[1][:, at])
            sides.append(mixed + pltpu.roll(mixed, 4, 0))
        return jnp.where(front, sides[0], sides[1])

    return jnp.where(last, 0.0, fold(0) - target * fold(16))


def near_kernel(second, sub_count, bucket_count, near_count, me_ref, work_ref, list_ref, *refs):
    refs = list(refs)
    tables = [refs.pop(0) for _ in range(sub_count * CHUNKS)]
    if second:
        table_refs = [refs.pop(0) for _ in range(sub_count)]
        acc_refs = [refs.pop(0) for _ in range(sub_count)]
    out_ref, tile_ref = refs[:2]
    refs = refs[2:]
    group_ref, sem = refs[:2]
    operands = [refs[2 + 4 * k : 6 + 4 * k] for k in range(4)]
    me = me_ref[0]
    mass_ref = group_ref
    if second:
        mass_ref, acc_ref = refs[2 + 4 * 4 :]
    piece = bucket_count // CHUNKS
    copies = [
        pltpu.make_async_copy(ref, mass_ref.at[pl.ds(k * piece, piece)], sem.at[k])
        for k, ref in enumerate(tables)
    ]
    if second:
        copies += [
            pltpu.make_async_copy(
                table_refs[k],
                group_ref.at[pl.ds(k * bucket_count, bucket_count)],
                sem.at[len(tables) + k],
            )
            for k in range(sub_count)
        ]
        copies += [
            pltpu.make_async_copy(acc_refs[k], acc_ref.at[k], sem.at[len(tables) + sub_count + k])
            for k in range(sub_count)
        ]
    for copy in copies:
        copy.start()
    for copy in copies:
        copy.wait()
    if second:
        last = row_iota() % 4 == 3
        for part in range(sub_count):

            @pl.loop(0, work_ref.shape[1], unroll=4)
            def _(i):
                slot = other_slot(work_ref[part, i], bucket_count, me)
                tile = group_ref[slot]
                act = jnp.where(last, tile, 0.0)
                act = act + pltpu.roll(act, 7, 0) + pltpu.roll(act, 6, 0) + pltpu.roll(act, 5, 0)
                group_ref[slot] = tile + (DT * DT) * act * acc_ref[part, i]

    def prepare(i, slot):
        tile = group_ref[other_slot(work_ref[0, i], bucket_count, me)]
        tile_ref[i] = tile
        slots = [list_ref[i, k] for k in range(near_count)]
        prepare_near(
            tile, [group_ref[n] for n in slots], [mass_ref[n] for n in slots], *operands[slot]
        )

    count = work_ref.shape[1]
    span = 4
    width = 2 * LANES
    rows = near_count * LANES
    prepare(0, 0)

    @pl.loop(0, pl.cdiv(count, span))
    def _(block):
        steps = [(part, start) for part in range(span) for start in range(0, rows, width)]
        first = block * span
        totals = {}

        def finish(part, start, dist):
            near_pulls(operands[part], start, width, dist, totals[part])
            if start + width == rows:
                target = operands[part][3][...]
                out_ref[jnp.minimum(first + part, count - 1)] = near_result(target, totals[part])

        pending = None
        for part, start in steps:
            if start == 0:
                totals[part] = [None, None]
            if start == width and part + 1 < span:
                prepare(jnp.minimum(first + part + 1, count - 1), part + 1)
            dist = near_distances(operands[part], start, width)
            if pending is not None:
                finish(*pending)
            pending = (part, start, dist)
        prepare(jnp.minimum(first + span, count - 1), 0)
        finish(*pending)


def splat_operand():
    shape = (PARTS, 7 * LANES)
    row = lax.broadcasted_iota(jnp.int32, shape, 0)
    number = lax.broadcasted_iota(jnp.int32, shape, 1) // LANES
    wanted = jnp.where(number == 0, 0, number + 3)
    keep = jnp.logical_and(row % ROWS == wanted, row < 3 * ROWS)
    return jnp.where(keep, 1.0, 0.0).astype(bf16)


def centre_operand():
    shape = (3 * ROWS, 6 * LANES)
    row = lax.broadcasted_iota(jnp.int32, shape, 0)
    number = lax.broadcasted_iota(jnp.int32, shape, 1) // (2 * LANES)
    return jnp.where(row % ROWS == number + 1, -1.0, 0.0).astype(bf16)


def cells_kernel(
    near_count,
    cell_count,
    top_count,
    list_ref,
    ess_ref,
    cells_ref,
    tile_ref,
    near_ref,
    out_ref,
    splat_ref,
    *slots,
):
    rows_ref = slots[4]
    build_rows(cells_ref, *slots[4:])
    splat_ref[...] = splat_operand()
    for side in range(2):
        slots[2 * side + 1][: 3 * ROWS, :] = centre_operand()
    count = tile_ref.shape[0]
    total = cell_count + top_count

    def pick_rows(i, slot, start, stop):
        picked_ref = slots[2 * slot]
        for k in range(start, stop):
            index = list_ref[i, near_count + k]
            if k < cell_count:
                index = ess_ref[index]
            picked_ref[pl.ds(k, 1), :] = rows_ref[pl.ds(index, 1), :]

    def place(i, slot):
        places_ref = slots[2 * slot + 1]
        parts = three(tile_ref[i])
        row = row_iota((ROWS, LANES))
        for half in range(2):
            for a in range(3):
                at = 4 * half + a
                spread = [jnp.broadcast_to(p[at : at + 1, :], (ROWS, LANES)) for p in parts]
                value = jnp.where(
                    row == 0,
                    spread[0],
                    jnp.where(row == 1, spread[1], jnp.where(row == 2, spread[2], 0.0)),
                )
                lanes = slice((2 * a + half) * LANES, (2 * a + half + 1) * LANES)
                places_ref[3 * ROWS :, lanes] = value.astype(bf16)

    def spread_cells(slot, start):
        picked_ref, places_ref = slots[2 * slot : 2 * slot + 2]
        left = picked_ref[start : start + CELL_CHUNK, :PARTS].astype(bf16)
        return (
            jnp.dot(left, splat_ref[...], preferred_element_type=f32),
            jnp.dot(left, places_ref[...], preferred_element_type=f32),
        )

    def finish(i, sums):
        row = row_iota()
        result = near_ref[i]
        for half in range(2):
            for a in range(3):
                value = jnp.sum(sums[half][a], axis=0, keepdims=True)
                value = jnp.broadcast_to(value, (8, LANES))
                result += jnp.where(row == 4 * half + a, value, 0.0)
        out_ref[i] = result

    pick_rows(0, 0, 0, total)
    place(0, 0)
    chunks = range(0, total, CELL_CHUNK)
    early = (len(chunks) - 1) * CELL_CHUNK // 8
    share = -(-total // early)

    @pl.loop(0, pl.cdiv(count, CELL_SPAN))
    def _(block):
        item = [jnp.minimum(CELL_SPAN * block + k, count - 1) for k in range(CELL_SPAN + 1)]
        waiting = spread_cells(0, 0)
        for step in range(CELL_SPAN):
            slot = step % 2
            sums = [[jnp.zeros((8, LANES), f32) for _ in range(3)] for _ in range(2)]
            done = 0
            place(item[step + 1], 1 - slot)
            for start in chunks:
                splats, offs = waiting
                if start + CELL_CHUNK < total:
                    waiting = spread_cells(slot, start + CELL_CHUNK)
                elif step + 1 < CELL_SPAN:
                    waiting = spread_cells(1 - slot, 0)
                for group in range(CELL_CHUNK // 8):
                    rows = slice(8 * group, 8 * group + 8)
                    number = [splats[rows, q * LANES : (q + 1) * LANES] for q in range(7)]
                    for half in range(2):
                        off = [
                            offs[rows, (2 * a + half) * LANES : (2 * a + half + 1) * LANES]
                            for a in range(3)
                        ]
                        cell_terms(off, number[0], number[1:], sums[half])
                    if done < total:
                        pick_rows(item[step + 1], 1 - slot, done, min(done + share, total))
                        done += share
            finish(item[step], sums)


def body(
    positions,
    velocities,
    masses,
    accel_prev,
    active,
    bucket_top,
    near_list,
    cell_list,
    top_list,
    essential,
    work,
):
    bucket_count = bucket_top.shape[0]
    sub_count = lax.axis_size("sub")
    dom_count = lax.axis_size("dom")
    me = lax.axis_index("sub").astype(jnp.int32)
    group_buckets = sub_count * bucket_count
    device_count = sub_count * dom_count
    near_count, cell_count, top_count = near_list.shape[1], cell_list.shape[1], top_list.shape[1]
    work_count = work.shape[0]
    vmem = pl.BlockSpec(memory_space=pltpu.VMEM)
    smem = pl.BlockSpec(memory_space=pltpu.SMEM)
    anywhere = pl.BlockSpec(memory_space=pl.ANY)
    work_shape = jax.ShapeDtypeStruct((work_count, 8, LANES), f32)
    sent_shape = jax.ShapeDtypeStruct((device_count * bucket_count // LANES * SENT, LANES), f32)

    activity = active.astype(f32)
    half_speed = velocities + 0.5 * DT * activity * accel_prev
    places = positions + DT * half_speed
    tiles = to_tiles(places, masses)
    places, half_speed, activity, _ = lax.optimization_barrier(
        (places, half_speed, activity, tiles)
    )
    ahead = to_tiles(places + DT * half_speed, activity)
    speeds = to_tiles(half_speed, activity)

    tops_row = bucket_top.astype(f32)[None]

    own = pl.pallas_call(
        first_moments_kernel,
        out_shape=sent_shape,
        in_specs=[vmem] * 2,
        out_specs=vmem,
        name="first_moments",
    )(tiles.reshape(-1, LANES), tops_row)

    def exchange(rows):
        wide = rows.reshape(device_count, -1)
        got = lax.all_to_all(wide, ("dom", "sub"), split_axis=0, concat_axis=0, tiled=True)
        return got.reshape(-1, LANES)

    cells = exchange(own)
    near_list, cell_list, top_list, essential, work, _ = lax.optimization_barrier(
        (near_list, cell_list, top_list, essential, work, own)
    )

    def as_rows(values):
        return jnp.pad(values, (0, -values.shape[0] % LANES)).reshape(-1, LANES)

    lists = jnp.concatenate([near_list, cell_list, top_list], axis=1)
    lists = jnp.pad(lists, ((0, 0), (0, -lists.shape[1] % LANES)))
    width = lists.shape[1]
    wanted = essential.reshape(dom_count, -1) + (
        jnp.arange(dom_count, dtype=jnp.int32) * group_buckets
    )[:, None]
    ess_size = wanted.size
    list_rows = bucket_count * width // LANES
    ess_rows = -(-ess_size // LANES)
    sent = jnp.concatenate(
        [lists.reshape(-1, LANES), as_rows(wanted.reshape(-1)), as_rows(work)], axis=0
    )
    sent_rows = sent.shape[0]
    sent = jnp.pad(sent, ((0, -sent_rows % 8), (0, 0)))
    all_rows = jnp.stack(sub_gather(sent, sub_count))
    ess_all = all_rows[:, list_rows : list_rows + ess_rows].reshape(sub_count, -1)
    ess_all = ess_all[:, :ess_size].reshape(-1)
    work_all = all_rows[:, list_rows + ess_rows : sent_rows].reshape(sub_count, -1)
    work_all = work_all[:, :work_count]
    mine = other_slot(work, bucket_count, me)
    if width == LANES:
        index = mine // bucket_count * sent.shape[0] + mine % bucket_count
        work_lists = jnp.take(all_rows.reshape(-1, LANES), index, axis=0)
    else:
        list_table = all_rows[:, :list_rows].reshape(group_buckets, width)
        work_lists = jnp.take(list_table, mine, axis=0)
    column = jnp.arange(width)[None]
    work_lists = jnp.where(
        column < near_count,
        other_slot(work_lists, bucket_count, me),
        jnp.where(
            column < near_count + cell_count,
            other_slot(work_lists, ess_size, me),
            work_lists + device_count * bucket_count,
        ),
    )
    piece = bucket_count // CHUNKS
    pieces = [sub_gather(tiles[c * piece : (c + 1) * piece], sub_count, work_lists) for c in range(CHUNKS)]
    table = [pieces[c][k] for k in range(sub_count) for c in range(CHUNKS)]
    ahead_sent, _ = lax.optimization_barrier((ahead, table))
    table_ahead = sub_gather(ahead_sent, sub_count)

    me_one = me[None]

    def near_call(second, extra_tables):
        operand = [
            pltpu.VMEM((near_count * LANES, 48), bf16),
            pltpu.VMEM((2, 48, 2 * LANES), bf16),
            pltpu.VMEM((32, near_count * LANES), bf16),
            pltpu.VMEM((8, LANES), f32),
        ]
        scratch = [
            pltpu.VMEM((group_buckets, 8, LANES), f32),
            pltpu.SemaphoreType.DMA(((2 + CHUNKS) * sub_count,)),
        ] + operand * 4
        specs = [smem] * 3 + [anywhere] * (sub_count * CHUNKS)
        if second:
            specs += [anywhere] * (2 * sub_count)
            scratch += [
                pltpu.VMEM((group_buckets, 8, LANES), f32),
                pltpu.VMEM((sub_count, work_count, 8, LANES), f32),
            ]
        return pl.pallas_call(
            functools.partial(near_kernel, second, sub_count, bucket_count, near_count),
            out_shape=(work_shape, work_shape),
            in_specs=specs,
            out_specs=(vmem, vmem),
            scratch_shapes=scratch,
            name="near_second" if second else "near_first",
        )(me_one, work_all, work_lists, *table, *extra_tables)

    def cells_call(cells, tile, near):
        buckets = cells.shape[0] // SENT * LANES
        scratch = [pltpu.VMEM((PARTS, 7 * LANES), bf16)] + [
            pltpu.VMEM((cell_count + top_count, LANES), f32),
            pltpu.VMEM((PARTS, 6 * LANES), bf16),
        ] * 2
        scratch += [
            pltpu.VMEM((buckets + TOP, LANES), f32),
            pltpu.VMEM((ROWS * buckets // LANES, LANES), f32),
            pltpu.VMEM((TOP // LANES * ROWS, LANES), f32),
            pltpu.VMEM((TOP // LANES * ROWS, LANES), f32),
        ]
        return pl.pallas_call(
            functools.partial(cells_kernel, near_count, cell_count, top_count),
            out_shape=work_shape,
            in_specs=[smem] * 2 + [vmem] * 3,
            out_specs=vmem,
            scratch_shapes=scratch,
            name="cell_force",
        )(work_lists, ess_all, cells, tile, near)

    near, tile = near_call(False, [])
    acc_one = sub_gather(cells_call(cells, tile, near), sub_count)
    flat_shape = jax.ShapeDtypeStruct((bucket_count * 8, LANES), f32)
    own_shape = jax.ShapeDtypeStruct(((bucket_count + 1) * 8, LANES), f32)

    def flat(values):
        return values.reshape(-1, LANES)

    own, places_two, base = pl.pallas_call(
        functools.partial(second_moments_kernel, sub_count),
        out_shape=(sent_shape, flat_shape, flat_shape),
        in_specs=[smem] * 2 + [vmem] * (4 + sub_count),
        out_specs=(vmem,) * 3,
        scratch_shapes=[pltpu.VMEM(own_shape.shape, f32)],
        name="second_moments",
    )(me_one, work_all, flat(ahead), flat(tiles), flat(speeds), tops_row, *acc_one)
    cells = exchange(own)
    near, tile = near_call(True, [*table_ahead, *acc_one])
    acc_two = sub_gather(cells_call(cells, tile, near), sub_count)
    speed_two = pl.pallas_call(
        functools.partial(final_kernel, sub_count),
        out_shape=flat_shape,
        in_specs=[smem] * 2 + [vmem] * (1 + sub_count),
        out_specs=vmem,
        scratch_shapes=[pltpu.VMEM(own_shape.shape, f32)],
        name="final_speeds",
    )(me_one, work_all, base, *acc_two)
    return (
        from_tiles(speed_two.reshape(-1, 8, LANES)),
        from_tiles(places_two.reshape(-1, 8, LANES)),
    )


def solution(mesh):
    both = ("dom", "sub")
    in_specs = (
        P(None, both),
        P(None, both),
        P(both),
        P(None, both),
        P(both),
        P(both),
        P(both, None),
        P(both, None),
        P(both, None),
        P("dom", "sub", None, None),
        P(both),
    )
    out_specs = (P(None, both), P(None, both))

    return jax.shard_map(body, mesh=mesh, in_specs=in_specs, out_specs=out_specs, check_vma=False)
```

profile of v0, /device:TPU:0, one launch (start us, length us, event | category | flops | bytes accessed | tf_op | source)
XLA Modules:
  0.0 140.7 jit_solution(15889699772515620362)
XLA Ops:
  0.7 0.6 copy-done.23
  1.3 0.6 convert_bitcast_fusion.tops_ref
  1.9 0.1 add.54
  2.0 0.9 broadcast_multiply_fusion
  3.0 1.7 %multiply_add_fusion.1 = (f32[3,32768]{1,0:T(4,128)S(1)}, f32[3,32768]{1,0:T(4,128)S(1)}) fusion(f32[3,32768]{1,0:T(4,128)} %param.11, f32[3,32768]{1,0:T(4,128)} %param.12, f32[3,32768]{1,0:T(4,128)} %param.14, f32[32768]{0:T(1024)S(1)} %broadcast_multiply_fusion), kind=kLoop, calls=%fused_computation.5 | loop fusion | flops 393216 | bytes 2097152 | tf_op jit(solution)/shard_map/add | solution.py:631
  4.7 1.1 pad_maximum_fusion.2
  5.8 2.1 %first_moments.1 = f32[352,128]{1,0:T(8,128)} custom-call(f32[1024,128]{1,0:T(8,128)} %bitcast.54, f32[1,128]{1,0:T(1,128)} %convert_bitcast_fusion.tops_ref), custom_call_target="tpu_custom_call" | custom-call | tf_op jit(solution)/shard_map/first_moments/pallas_call | solution.py:641
  8.0 0.1 reshape.81
  8.0 0.1 copy.38
  8.2 0.1 copy.39
  8.3 0.1 copy.40
  8.4 0.1 pad_add_fusion.2
  8.5 3.1 %collective-permute-start.1 = (s32[136,128]{1,0:T(8,128)S(1)}, s32[136,128]{1,0:T(8,128)S(1)}, u32[]{:S(2)}, u32[]{:S(2)}) collective-permute-start(s32[136,128]{1,0:T(8,128)S(1)} %pad.14), channel_id=1, source_target_pairs={{0,2},{1,3},{2,0},{3,1},{4,6},{5,7},{6,4},{7,5},{8,10},{9,11},{10,... | collective-permute-start | bytes 208904 | tf_op jit(solution)/shard_map/ppermute | solution.py:53
  11.6 0.4 collective-permute-start.4
  12.0 0.1 collective-permute-start.3
  12.2 2.0 %collective-permute-done.1 = s32[136,128]{1,0:T(8,128)S(1)} collective-permute-done((s32[136,128]{1,0:T(8,128)S(1)}, s32[136,128]{1,0:T(8,128)S(1)}, u32[]{:S(2)}, u32[]{:S(2)}) %collective-permute-start.1) | collective-permute-done | bytes 69664 | tf_op jit(solution)/shard_map/ppermute | solution.py:53
  14.2 1.2 collective-permute-done.2
  15.4 0.3 pad_add_fusion
  15.7 0.6 gather_fusion
  16.3 0.7 select_select_fusion.list_ref
  17.0 9.0 %collective-permute-done.4.refs_2_ = f32[128,8,128]{2,1,0:T(8,128)S(1)} collective-permute-done((f32[128,8,128]{2,1,0:T(8,128)S(1)}, f32[128,8,128]{2,1,0:T(8,128)S(1)}, u32[]{:S(2)}, u32[]{:S(2)}) %collective-permute-start.4) | collective-permute-done | bytes 524320 | tf_op jit(solution)/shard_map/ppermute | solution.py:53
  25.9 0.2 multiply_add_fusion
  26.1 0.6 copy-done.2
  26.7 1.1 pad_maximum_fusion
  27.9 1.1 collective-permute-start.10
  29.0 5.3 %all-to-all-start = ((f32[32,1,1408]{2,1,0:T(1,128)}), f32[32,1,1408]{2,1,0:T(1,128)S(1)}, u32[]{:S(2)}, u32[]{:S(2)}) async-start(f32[32,1,1408]{2,1,0:T(1,128)} %bitcast.68), calls=%async_computation | async-start | bytes 360448 | tf_op jit(solution)/shard_map/all_to_all | solution.py:651
  34.3 0.6 copy.47
  34.9 0.6 slice_bitcast_fusion
  35.5 17.6 %near_first.1 = (f32[40,8,128]{2,1,0:T(8,128)}, f32[40,8,128]{2,1,0:T(8,128)}) custom-call(s32[1]{0:T(128)} %bitcast.me_ref, s32[4,40]{1,0:T(4,128)} %bitcast.80, s32[40,128]{1,0:T(8,128)} %select_select_fusion.list_ref, f32[128,8,128]{2,1,0:T(8,128)} %bitcast.55, f32[128,8,128]{2,1,0:T(8,128)} %copy-done.3, f32[128,8,128]{2,1,0:T(8,128)} %copy-done.2, ...), custom_call_target="tpu_custom_call" | custom-call | tf_op jit(solution)/shard_map/near_first/pallas_call | solution.py:724
  53.1 0.7 copy-done.6
  53.8 17.5 %cell_force.2.refs_0_.refs_8_ = f32[40,8,128]{2,1,0:T(8,128)} custom-call(s32[40,128]{1,0:T(8,128)} %select_select_fusion.list_ref, s32[1024]{0:T(1024)} %bitcast.84, f32[352,128]{1,0:T(8,128)} %bitcast.70, f32[40,8,128]{2,1,0:T(8,128)} %get-tuple-element.28.tile_ref, f32[40,8,128]{2,1,0:T(8,128)} %get-tuple-element.29.near_ref), custom_call_target="tpu_custom_call" | custom-call | tf_op jit(solution)/shard_map/cell_force/pallas_call | solution.py:745
  71.3 1.7 %collective-permute-start.7 = (f32[40,8,128]{2,1,0:T(8,128)}, f32[40,8,128]{2,1,0:T(8,128)S(1)}, u32[]{:S(2)}, u32[]{:S(2)}) collective-permute-start(f32[40,8,128]{2,1,0:T(8,128)} %cell_force.2.refs_0_.refs_8_), channel_id=1, source_target_pairs={{0,2},{1,3},{2,0},{3,1},{4,6},{5,7},{6,4},{7,5},{8,10},{9,11},{10,... | collective-permute-start | bytes 491528 | tf_op jit(solution)/shard_map/ppermute | solution.py:53
  73.1 0.5 collective-permute-start.11
  73.7 4.2 %collective-permute-done.7.refs_2_.refs_10_ = f32[40,8,128]{2,1,0:T(8,128)S(1)} collective-permute-done((f32[40,8,128]{2,1,0:T(8,128)}, f32[40,8,128]{2,1,0:T(8,128)S(1)}, u32[]{:S(2)}, u32[]{:S(2)}) %collective-permute-start.7) | collective-permute-done | bytes 163872 | tf_op jit(solution)/shard_map/ppermute | solution.py:53
  77.9 1.4 collective-permute-done.8.refs_3_.refs_11_
  79.3 0.7 copy-done.9
  79.9 3.5 %second_moments.1 = (f32[352,128]{1,0:T(8,128)}, f32[1024,128]{1,0:T(8,128)}, f32[1024,128]{1,0:T(8,128)}) custom-call(s32[1]{0:T(128)} %bitcast.me_ref, s32[4,40]{1,0:T(4,128)} %bitcast.81, f32[1024,128]{1,0:T(8,128)} %bitcast.64, f32[1024,128]{1,0:T(8,128)} %bitcast.56, f32[1024,128]{1,0:T(8,128)} %bitcast.66, f32[1,128]{1,0:T(1,128)} %convert_bitcast_fusion.tops_ref, ...), custom_call_target="tpu_custom_call" | custom-call | tf_op jit(solution)/shard_map/second_moments/pallas_call | solution.py:762
  83.5 5.9 %all-to-all-start.1 = ((f32[32,1,1408]{2,1,0:T(1,128)}), f32[32,1,1408]{2,1,0:T(1,128)S(1)}, u32[]{:S(2)}, u32[]{:S(2)}) async-start(f32[32,1,1408]{2,1,0:T(1,128)} %bitcast.75), calls=%async_computation.1 | async-start | bytes 360448 | tf_op jit(solution)/shard_map/all_to_all | solution.py:651
  89.4 0.8 copy-done.12
  90.1 0.8 copy-done.13
  90.9 20.0 %near_second.1 = (f32[40,8,128]{2,1,0:T(8,128)}, f32[40,8,128]{2,1,0:T(8,128)}) custom-call(s32[1]{0:T(128)} %bitcast.me_ref, s32[4,40]{1,0:T(4,128)} %bitcast.82, s32[40,128]{1,0:T(8,128)} %select_select_fusion.list_ref, f32[128,8,128]{2,1,0:T(8,128)} %bitcast.57, f32[128,8,128]{2,1,0:T(8,128)} %copy-done.3, f32[128,8,128]{2,1,0:T(8,128)} %copy-done.2, ...), custom_call_target="tpu_custom_call" | custom-call | tf_op jit(solution)/shard_map/near_second/pallas_call | solution.py:724
  111.0 0.7 copy-done.5
  111.7 17.5 %cell_force.3.refs_0_ = f32[40,8,128]{2,1,0:T(8,128)} custom-call(s32[40,128]{1,0:T(8,128)} %select_select_fusion.list_ref, s32[1024]{0:T(1024)} %bitcast.85, f32[352,128]{1,0:T(8,128)} %bitcast.69, f32[40,8,128]{2,1,0:T(8,128)} %get-tuple-element.33.tile_ref, f32[40,8,128]{2,1,0:T(8,128)} %get-tuple-element.34.near_ref), custom_call_target="tpu_custom_call" | custom-call | tf_op jit(solution)/shard_map/cell_force/pallas_call | solution.py:745
  129.2 1.6 %collective-permute-start.13 = (f32[40,8,128]{2,1,0:T(8,128)}, f32[40,8,128]{2,1,0:T(8,128)S(1)}, u32[]{:S(2)}, u32[]{:S(2)}) collective-permute-start(f32[40,8,128]{2,1,0:T(8,128)} %cell_force.3.refs_0_), channel_id=1, source_target_pairs={{0,2},{1,3},{2,0},{3,1},{4,6},{5,7},{6,4},{7,5},{8,10},{9,11},{10,... | collective-permute-start | bytes 491528 | tf_op jit(solution)/shard_map/ppermute | solution.py:53
  130.8 4.8 %collective-permute-done.13.refs_2_ = f32[40,8,128]{2,1,0:T(8,128)S(1)} collective-permute-done((f32[40,8,128]{2,1,0:T(8,128)}, f32[40,8,128]{2,1,0:T(8,128)S(1)}, u32[]{:S(2)}, u32[]{:S(2)}) %collective-permute-start.13) | collective-permute-done | bytes 163872 | tf_op jit(solution)/shard_map/ppermute | solution.py:53
  135.6 1.4 collective-permute-done.14.refs_3_
  137.0 0.7 copy-done.16
  137.7 3.1 %final_speeds.1 = f32[1024,128]{1,0:T(8,128)} custom-call(s32[1]{0:T(128)} %bitcast.me_ref, s32[4,40]{1,0:T(4,128)} %bitcast.83, f32[1024,128]{1,0:T(8,128)} %get-tuple-element.30.base_ref, f32[40,8,128]{2,1,0:T(8,128)} %cell_force.3.refs_0_, f32[40,8,128]{2,1,0:T(8,128)} %copy-done.15, f32[40,8,128]{2,1,0:T(8,128)} %copy-done.14, f32[40,8,128]{2,1,0:T(8,128)} %copy-done.16), custom_call_target="tpu_custom_call" | custom-call | tf_op jit(solution)/shard_map/final_speeds/pallas_call | solution.py:773
  (70 shorter events, 0.4 us)
Async XLA Ops:
  0.6 0.7 copy-start.23
  3.0 1.7 %copy-start.17 = (f32[32768]{0:T(1024)S(1)}, f32[32768]{0:T(1024)}, u32[]{:S(2)}) copy-start(f32[32768]{0:T(1024)} %param.13) | copy-start | bytes 393220
  5.8 2.2 %copy-start.22 = (s32[40]{0:T(128)S(1)}, s32[40]{0:T(128)}, u32[]{:S(2)}) copy-start(s32[40]{0:T(128)} %param.21) | copy-start | bytes 484
  5.8 2.2 %copy-start.20 = (s32[1,1,8,32]{3,2,1,0:T(8,128)S(1)}, s32[1,1,8,32]{3,2,1,0:T(8,128)}, u32[]{:S(2)}) copy-start(s32[1,1,8,32]{3,2,1,0:T(8,128)} %param.20) | copy-start | bytes 3076
  5.8 2.3 %copy-start.21 = (s32[128,4]{0,1:T(4,128)S(1)}, s32[128,4]{0,1:T(4,128)}, u32[]{:S(2)}) copy-start(s32[128,4]{0,1:T(4,128)} %param.17) | copy-start | bytes 6148
  5.8 2.4 %copy-start.18 = (s32[128,64]{0,1:T(8,128)S(1)}, s32[128,64]{0,1:T(8,128)}, u32[]{:S(2)}) copy-start(s32[128,64]{0,1:T(8,128)} %param.18) | copy-start | bytes 98308
  5.8 2.5 %copy-start.19 = (s32[128,32]{0,1:T(8,128)S(1)}, s32[128,32]{0,1:T(8,128)}, u32[]{:S(2)}) copy-start(s32[128,32]{0,1:T(8,128)} %param.19) | copy-start | bytes 49156
  7.9 3.6 %copy-start = (f32[4,128,2,128]{3,0,2,1:T(4,128)S(1)}, f32[4,128,2,128]{3,0,2,1:T(4,128)}, u32[]{:S(2)}) copy-start(f32[4,128,2,128]{3,0,2,1:T(4,128)} %pad_maximum_fusion.2) | copy-start | bytes 1572868
  8.5 3.6 %copy-start.10 = (s32[32768]{0:T(1024)S(1)}, s32[32768]{0:T(1024)}, u32[]{:S(2)}) copy-start(s32[32768]{0:T(1024)} %param.15) | copy-start | bytes 393220
  8.5 5.6 %collective-permute-start.1 = (s32[136,128]{1,0:T(8,128)S(1)}, s32[136,128]{1,0:T(8,128)S(1)}, u32[]{:S(2)}, u32[]{:S(2)}) collective-permute-start(s32[136,128]{1,0:T(8,128)S(1)} %pad.14), channel_id=1, source_target_pairs={{0,2},{1,3},{2,0},{3,1},{4,6},{5,7},{6,4},{7,5},{8,10},{9,11},{10,... | collective-permute-start | bytes 208904 | tf_op jit(solution)/shard_map/ppermute | solution.py:53
  11.6 2.6 %collective-permute-start = (s32[136,128]{1,0:T(8,128)S(1)}, s32[136,128]{1,0:T(8,128)S(1)}, u32[]{:S(2)}, u32[]{:S(2)}) collective-permute-start(s32[136,128]{1,0:T(8,128)S(1)} %pad.14), channel_id=1, source_target_pairs={{0,1},{1,0},{2,3},{3,2},{4,5},{5,4},{6,7},{7,6},{8,9},{9,8},{10,11... | collective-permute-start | bytes 208904 | tf_op jit(solution)/shard_map/ppermute | solution.py:57
  11.6 14.3 %collective-permute-start.4 = (f32[128,8,128]{2,1,0:T(8,128)S(1)}, f32[128,8,128]{2,1,0:T(8,128)S(1)}, u32[]{:S(2)}, u32[]{:S(2)}) collective-permute-start(f32[128,8,128]{2,1,0:T(8,128)S(1)} %bitcast.58), channel_id=1, source_target_pairs={{0,2},{1,3},{2,0},{3,1},{4,6},{5,7},{6,4},{7,5},{8,10},{9,11},{10,... | collective-permute-start | bytes 1572872 | tf_op jit(solution)/shard_map/ppermute | solution.py:53
  12.0 15.9 %collective-permute-start.3 = (f32[128,8,128]{2,1,0:T(8,128)S(1)}, f32[128,8,128]{2,1,0:T(8,128)S(1)}, u32[]{:S(2)}, u32[]{:S(2)}) collective-permute-start(f32[128,8,128]{2,1,0:T(8,128)S(1)} %bitcast.59), channel_id=1, source_target_pairs={{0,1},{1,0},{2,3},{3,2},{4,5},{5,4},{6,7},{7,6},{8,9},{9,8},{10,11... | collective-permute-start | bytes 1572872 | tf_op jit(solution)/shard_map/ppermute | solution.py:57
  14.2 1.3 collective-permute-start.2
  25.9 0.8 copy-start.2
  25.9 1.9 %collective-permute-start.5 = (f32[128,8,128]{2,1,0:T(8,128)S(1)}, f32[128,8,128]{2,1,0:T(8,128)S(1)}, u32[]{:S(2)}, u32[]{:S(2)}) collective-permute-start(f32[128,8,128]{2,1,0:T(8,128)S(1)} %collective-permute-done.4.refs_2_), channel_id=1, source_target_pairs={{0,1},{1,0},{2,3},{3,2},{4,5},{5,4},{6,7},{7,6},{8,9},{9,8},{10,11... | collective-permute-start | bytes 1572872 | tf_op jit(solution)/shard_map/ppermute | solution.py:57
  27.9 45.2 %copy-start.1 = (f32[4,128,2,128]{3,0,2,1:T(4,128)}, f32[4,128,2,128]{3,0,2,1:T(4,128)S(1)}, u32[]{:S(2)}) copy-start(f32[4,128,2,128]{3,0,2,1:T(4,128)S(1)} %get-tuple-element.41) | copy-start | bytes 1572868
  27.9 7.6 %copy-start.3 = (f32[128,8,128]{2,1,0:T(8,128)}, f32[128,8,128]{2,1,0:T(8,128)S(1)}, u32[]{:S(2)}) copy-start(f32[128,8,128]{2,1,0:T(8,128)S(1)} %collective-permute-done.3.refs_1_) | copy-start | bytes 1572868
  27.9 7.6 %copy-start.4 = (f32[128,8,128]{2,1,0:T(8,128)}, f32[128,8,128]{2,1,0:T(8,128)S(1)}, u32[]{:S(2)}) copy-start(f32[128,8,128]{2,1,0:T(8,128)S(1)} %collective-permute-done.5.refs_3_) | copy-start | bytes 1572868
  27.9 45.2 %collective-permute-start.10 = (f32[128,8,128]{2,1,0:T(8,128)S(1)}, f32[128,8,128]{2,1,0:T(8,128)S(1)}, u32[]{:S(2)}, u32[]{:S(2)}) collective-permute-start(f32[128,8,128]{2,1,0:T(8,128)S(1)} %bitcast.62), channel_id=1, source_target_pairs={{0,2},{1,3},{2,0},{3,1},{4,6},{5,7},{6,4},{7,5},{8,10},{9,11},{10,... | collective-permute-start | bytes 1572872 | tf_op jit(solution)/shard_map/ppermute | solution.py:53
  29.0 24.1 %all-to-all-start = ((f32[32,1,1408]{2,1,0:T(1,128)}), f32[32,1,1408]{2,1,0:T(1,128)S(1)}, u32[]{:S(2)}, u32[]{:S(2)}) async-start(f32[32,1,1408]{2,1,0:T(1,128)} %bitcast.68), calls=%async_computation | async-start | bytes 360448 | tf_op jit(solution)/shard_map/all_to_all | solution.py:651
  53.1 0.7 copy-start.6
  71.3 6.6 %collective-permute-start.7 = (f32[40,8,128]{2,1,0:T(8,128)}, f32[40,8,128]{2,1,0:T(8,128)S(1)}, u32[]{:S(2)}, u32[]{:S(2)}) collective-permute-start(f32[40,8,128]{2,1,0:T(8,128)} %cell_force.2.refs_0_.refs_8_), channel_id=1, source_target_pairs={{0,2},{1,3},{2,0},{3,1},{4,6},{5,7},{6,4},{7,5},{8,10},{9,11},{10,... | collective-permute-start | bytes 491528 | tf_op jit(solution)/shard_map/ppermute | solution.py:53
  73.1 16.3 %collective-permute-start.9 = (f32[128,8,128]{2,1,0:T(8,128)S(1)}, f32[128,8,128]{2,1,0:T(8,128)S(1)}, u32[]{:S(2)}, u32[]{:S(2)}) collective-permute-start(f32[128,8,128]{2,1,0:T(8,128)S(1)} %bitcast.63), channel_id=1, source_target_pairs={{0,1},{1,0},{2,3},{3,2},{4,5},{5,4},{6,7},{7,6},{8,9},{9,8},{10,11... | collective-permute-start | bytes 1572872 | tf_op jit(solution)/shard_map/ppermute | solution.py:57
  73.1 16.3 %copy-start.11 = (f32[128,8,128]{2,1,0:T(8,128)}, f32[128,8,128]{2,1,0:T(8,128)S(1)}, u32[]{:S(2)}) copy-start(f32[128,8,128]{2,1,0:T(8,128)S(1)} %collective-permute-done.10.refs_6_) | copy-start | bytes 1572868
  73.1 16.3 %collective-permute-start.11 = (f32[128,8,128]{2,1,0:T(8,128)S(1)}, f32[128,8,128]{2,1,0:T(8,128)S(1)}, u32[]{:S(2)}, u32[]{:S(2)}) collective-permute-start(f32[128,8,128]{2,1,0:T(8,128)S(1)} %collective-permute-done.10.refs_6_), channel_id=1, source_target_pairs={{0,1},{1,0},{2,3},{3,2},{4,5},{5,4},{6,7},{7,6},{8,9},{9,8},{10,11... | collective-permute-start | bytes 1572872 | tf_op jit(solution)/shard_map/ppermute | solution.py:57
  73.6 4.3 %collective-permute-start.6 = (f32[40,8,128]{2,1,0:T(8,128)}, f32[40,8,128]{2,1,0:T(8,128)S(1)}, u32[]{:S(2)}, u32[]{:S(2)}) collective-permute-start(f32[40,8,128]{2,1,0:T(8,128)} %cell_force.2.refs_0_.refs_8_), channel_id=1, source_target_pairs={{0,1},{1,0},{2,3},{3,2},{4,5},{5,4},{6,7},{7,6},{8,9},{9,8},{10,11... | collective-permute-start | bytes 491528 | tf_op jit(solution)/shard_map/ppermute | solution.py:57
  77.9 1.4 copy-start.7
  77.9 1.4 collective-permute-start.8
  77.9 1.4 copy-start.8
  79.3 0.7 copy-start.9
  83.5 27.5 %all-to-all-start.1 = ((f32[32,1,1408]{2,1,0:T(1,128)}), f32[32,1,1408]{2,1,0:T(1,128)S(1)}, u32[]{:S(2)}, u32[]{:S(2)}) async-start(f32[32,1,1408]{2,1,0:T(1,128)} %bitcast.75), calls=%async_computation.1 | async-start | bytes 360448 | tf_op jit(solution)/shard_map/all_to_all | solution.py:651
  89.3 0.8 copy-start.12
  90.1 0.8 copy-start.13
  111.0 0.7 copy-start.5
  129.2 6.4 %collective-permute-start.13 = (f32[40,8,128]{2,1,0:T(8,128)}, f32[40,8,128]{2,1,0:T(8,128)S(1)}, u32[]{:S(2)}, u32[]{:S(2)}) collective-permute-start(f32[40,8,128]{2,1,0:T(8,128)} %cell_force.3.refs_0_), channel_id=1, source_target_pairs={{0,2},{1,3},{2,0},{3,1},{4,6},{5,7},{6,4},{7,5},{8,10},{9,11},{10,... | collective-permute-start | bytes 491528 | tf_op jit(solution)/shard_map/ppermute | solution.py:53
  130.8 4.8 %collective-permute-start.12 = (f32[40,8,128]{2,1,0:T(8,128)}, f32[40,8,128]{2,1,0:T(8,128)S(1)}, u32[]{:S(2)}, u32[]{:S(2)}) collective-permute-start(f32[40,8,128]{2,1,0:T(8,128)} %cell_force.3.refs_0_), channel_id=1, source_target_pairs={{0,1},{1,0},{2,3},{3,2},{4,5},{5,4},{6,7},{7,6},{8,9},{9,8},{10,11... | collective-permute-start | bytes 491528 | tf_op jit(solution)/shard_map/ppermute | solution.py:57
  135.6 1.4 copy-start.14
  135.6 1.4 collective-permute-start.14
  135.6 1.4 copy-start.15
  137.0 0.7 copy-start.16
where the time goes:
time: 141 us
  Pallas kernels  81.4 us (58%)
  waiting for transfers between devices  24 us (17%)
  starting transfers between devices  19.8 us (14%)
  local copies, waits for them, and re-layouts  7.83 us (6%)
  other arithmetic  6.73 us (5%)
    pallas_call x2, Pallas kernels, near_call(): pl.pallas_call(functools.partial(near_kernel, second, sub_count, bucket_c...  37.6 us
    pallas_call x2, Pallas kernels, cells_call(): pl.pallas_call(functools.partial(cells_kernel, near_count, cell_count, to...  35.1 us
    ppermute x5, waiting for transfers between devices, sub_gather(): lax.ppermute(block, 'sub', [(i, i ^ step) for i in range(sub_count)])  20 us
    all_to_all x2, starting transfers between devices, exchange(): lax.all_to_all(wide, ('dom', 'sub'), split_axis=0, concat_axis=0, tiled=T...  11.2 us
    ppermute x5, starting transfers between devices, sub_gather(): lax.ppermute(block, 'sub', [(i, i ^ step) for i in range(sub_count)])  7.86 us
    unnamed x48, local copies, waits for them, and re-layouts  5.52 us
    ppermute x10, waiting for transfers between devices, sub_gather(): lax.ppermute(parts[step], 'sub', [(i, i ^ 1) for i in range(sub_count)])  4.02 us
    pallas_call x1, Pallas kernels, body(): pl.pallas_call(functools.partial(second_moments_kernel, sub_count), out_s...  3.53 us
  transfers between devices with their start and end apart: 17, of which 7 were waited for; matrix products, arithmetic and copies ran while one was open for 3% of the time, Pallas kernels for 42%

commit v1 on v0

--- a/solution.py
+++ b/solution.py
@@ -405,11 +405,11 @@
     out_ref, tile_ref = refs[:2]
     refs = refs[2:]
     group_ref, sem = refs[:2]
-    operands = [refs[2 + 4 * k : 6 + 4 * k] for k in range(4)]
+    operands = [refs[2 + 4 * k : 6 + 4 * k] for k in range(8)]
     me = me_ref[0]
     mass_ref = group_ref
     if second:
-        mass_ref, acc_ref = refs[2 + 4 * 4 :]
+        mass_ref, acc_ref = refs[2 + 4 * 8 :]
     piece = bucket_count // CHUNKS
     copies = [
         pltpu.make_async_copy(ref, mass_ref.at[pl.ds(k * piece, piece)], sem.at[k])
@@ -453,7 +453,7 @@
         )
 
     count = work_ref.shape[1]
-    span = 4
+    span = 8
     width = 2 * LANES
     rows = near_count * LANES
     prepare(0, 0)
@@ -643,6 +643,7 @@
         out_shape=sent_shape,
         in_specs=[vmem] * 2,
         out_specs=vmem,
+        compiler_params=pltpu.CompilerParams(vmem_limit_bytes=20 << 20),
         name="first_moments",
     )(tiles.reshape(-1, LANES), tops_row)
 
@@ -713,7 +714,7 @@
         scratch = [
             pltpu.VMEM((group_buckets, 8, LANES), f32),
             pltpu.SemaphoreType.DMA(((2 + CHUNKS) * sub_count,)),
-        ] + operand * 4
+        ] + operand * 8
         specs = [smem] * 3 + [anywhere] * (sub_count * CHUNKS)
         if second:
             specs += [anywhere] * (2 * sub_count)
@@ -727,6 +728,7 @@
             in_specs=specs,
             out_specs=(vmem, vmem),
             scratch_shapes=scratch,
+            compiler_params=pltpu.CompilerParams(vmem_limit_bytes=20 << 20),
             name="near_second" if second else "near_first",
         )(me_one, work_all, work_lists, *table, *extra_tables)
 
@@ -765,6 +767,7 @@
         in_specs=[smem] * 2 + [vmem] * (4 + sub_count),
         out_specs=(vmem,) * 3,
         scratch_shapes=[pltpu.VMEM(own_shape.shape, f32)],
+        compiler_params=pltpu.CompilerParams(vmem_limit_bytes=20 << 20),
         name="second_moments",
     )(me_one, work_all, flat(ahead), flat(tiles), flat(speeds), tops_row, *acc_one)
     cells = exchange(own)
@@ -776,6 +779,7 @@
         in_specs=[smem] * 2 + [vmem] * (1 + sub_count),
         out_specs=vmem,
         scratch_shapes=[pltpu.VMEM(own_shape.shape, f32)],
+        compiler_params=pltpu.CompilerParams(vmem_limit_bytes=20 << 20),
         name="final_speeds",
     )(me_one, work_all, base, *acc_two)
     return (

time: 141 us -> 134 us (0.950)
  Pallas kernels: 81.4 us -> 72.6 us
  local copies, waits for them, and re-layouts: 7.83 us -> 10.3 us
    pallas_call x2, Pallas kernels: 37.6 us -> 31.7 us  [near_call(): pl.pallas_call(functools.partial(near_kernel, second, sub_count, bucket_c...]
    unnamed x48, local copies, waits for them, and re-layouts: 5.52 us -> 8.54 us
  transfers between devices with their start and end apart: 17 -> 17, of which waited for: 7 -> 8; matrix products, arithmetic and copies ran while one was open for 3% -> 3% of each run, Pallas kernels for 42% -> 39%
where the time goes in v1:
time: 134 us
  Pallas kernels  72.6 us (54%)
  waiting for transfers between devices  24.3 us (18%)
  starting transfers between devices  19.8 us (15%)
  local copies, waits for them, and re-layouts  10.3 us (8%)
  other arithmetic  5.6 us (4%)
    pallas_call x2, Pallas kernels, cells_call(): pl.pallas_call(functools.partial(cells_kernel, near_count, cell_count, to...  35.2 us
    pallas_call x2, Pallas kernels, near_call(): pl.pallas_call(functools.partial(near_kernel, second, sub_count, bucket_c...  31.7 us
    ppermute x5, waiting for transfers between devices, sub_gather(): lax.ppermute(block, 'sub', [(i, i ^ step) for i in range(sub_count)])  19.9 us
    all_to_all x2, starting transfers between devices, exchange(): lax.all_to_all(wide, ('dom', 'sub'), split_axis=0, concat_axis=0, tiled=T...  11.5 us
    unnamed x48, local copies, waits for them, and re-layouts  8.54 us
    ppermute x5, starting transfers between devices, sub_gather(): lax.ppermute(block, 'sub', [(i, i ^ step) for i in range(sub_count)])  7.49 us
    ppermute x10, waiting for transfers between devices, sub_gather(): lax.ppermute(parts[step], 'sub', [(i, i ^ 1) for i in range(sub_count)])  4.34 us
  transfers between devices with their start and end apart: 17, of which 8 were waited for; matrix products, arithmetic and copies ran while one was open for 3% of the time, Pallas kernels for 39%

profile of v1, /device:TPU:0, one launch (start us, length us, event | category | flops | bytes accessed | tf_op | source)
XLA Modules:
  0.0 133.5 jit_solution(14819055817028339291)
XLA Ops:
  0.7 0.6 copy-done.23
  1.4 0.9 broadcast_multiply_fusion
  2.4 1.7 %multiply_add_fusion.1 = (f32[3,32768]{1,0:T(4,128)S(1)}, f32[3,32768]{1,0:T(4,128)S(1)}) fusion(f32[3,32768]{1,0:T(4,128)} %param.11, f32[3,32768]{1,0:T(4,128)} %param.12, f32[3,32768]{1,0:T(4,128)} %param.14, f32[32768]{0:T(1024)S(1)} %broadcast_multiply_fusion), kind=kLoop, calls=%fused_computation.5 | loop fusion | flops 393216 | bytes 2097152 | tf_op jit(solution)/shard_map/add | solution.py:631
  4.1 0.2 pad_maximum_fusion.2
  4.4 1.0 first_moments.1
  5.5 0.6 copy-done.21
  6.1 0.1 copy.38
  6.2 0.6 copy-done.18
  7.0 0.6 copy-done.19
  7.6 0.1 copy.40
  7.7 0.1 pad_add_fusion.2
  7.9 3.1 %collective-permute-start.1 = (s32[136,128]{1,0:T(8,128)S(1)}, s32[136,128]{1,0:T(8,128)S(1)}, u32[]{:S(2)}, u32[]{:S(2)}) collective-permute-start(s32[136,128]{1,0:T(8,128)S(1)} %pad.14), channel_id=1, source_target_pairs={{0,2},{1,3},{2,0},{3,1},{4,6},{5,7},{6,4},{7,5},{8,10},{9,11},{10,... | collective-permute-start | bytes 208904 | tf_op jit(solution)/shard_map/ppermute | solution.py:53
  10.9 0.2 collective-permute-start.4
  11.1 0.4 collective-permute-start.3
  11.4 0.7 convert_element_type.6
  12.1 1.4 %collective-permute-done.1 = s32[136,128]{1,0:T(8,128)S(1)} collective-permute-done((s32[136,128]{1,0:T(8,128)S(1)}, s32[136,128]{1,0:T(8,128)S(1)}, u32[]{:S(2)}, u32[]{:S(2)}) %collective-permute-start.1) | collective-permute-done | bytes 69664 | tf_op jit(solution)/shard_map/ppermute | solution.py:53
  13.5 1.2 collective-permute-done.2
  14.8 0.3 pad_add_fusion
  15.0 0.6 gather_fusion
  15.7 9.5 %collective-permute-done.4.refs_2_ = f32[128,8,128]{2,1,0:T(8,128)S(1)} collective-permute-done((f32[128,8,128]{2,1,0:T(8,128)S(1)}, f32[128,8,128]{2,1,0:T(8,128)S(1)}, u32[]{:S(2)}, u32[]{:S(2)}) %collective-permute-start.4) | collective-permute-done | bytes 524320 | tf_op jit(solution)/shard_map/ppermute | solution.py:53
  25.3 0.2 multiply_add_fusion
  25.5 1.4 %pad_maximum_fusion = (f32[4,128,2,128]{3,0,2,1:T(4,128)S(1)}, f32[4,128,2,128]{3,0,2,1:T(4,128)S(1)}) fusion(f32[1,128,2,128]{3,0,2,1:T(1,128)S(1)} %bitcast.75, f32[3,128,2,128]{3,0,2,1:T(4,128)} %bitcast.70, f32[3,128,2,128]{3,0,2,1:T(4,128)S(1)} %bitcast.72), kind=kLoop, calls=%fused_computation.1 | loop fusion | flops 262144 | bytes 1966080 | tf_op jit(solution)/shard_map/concatenate | solution.py:37
  26.9 0.3 collective-permute-done.5.refs_3_
  27.2 1.0 collective-permute-start.10
  28.2 5.4 %all-to-all-start = ((f32[32,1,1408]{2,1,0:T(1,128)}), f32[32,1,1408]{2,1,0:T(1,128)}, u32[]{:S(2)}, u32[]{:S(2)}) async-start(f32[32,1,1408]{2,1,0:T(1,128)} %bitcast.26), calls=%async_computation | async-start | bytes 360448 | tf_op jit(solution)/shard_map/all_to_all | solution.py:652
  33.7 0.6 copy.47
  34.3 14.4 %near_first.1 = (f32[40,8,128]{2,1,0:T(8,128)S(1)}, f32[40,8,128]{2,1,0:T(8,128)S(1)}) custom-call(s32[1]{0:T(128)} %bitcast.me_ref, s32[4,40]{1,0:T(4,128)S(1)} %bitcast.66, s32[40,128]{1,0:T(8,128)S(1)} %select_select_fusion.list_ref, f32[128,8,128]{2,1,0:T(8,128)S(1)} %bitcast.57, f32[128,8,128]{2,1,0:T(8,128)S(1)} %collective-permute-done.3.refs_1_, ...), custom_call_target="tpu_custom_call" | custom-call | tf_op jit(solution)/shard_map/near_first/pallas_call | solution.py:725
  48.7 0.6 copy-done.12
  49.3 0.7 copy-done.13
  50.0 17.6 %cell_force.2.refs_0_.refs_8_ = f32[40,8,128]{2,1,0:T(8,128)} custom-call(s32[40,128]{1,0:T(8,128)} %copy-done.7, s32[1024]{0:T(1024)} %bitcast.81, f32[352,128]{1,0:T(8,128)} %bitcast.27.cells_ref, f32[40,8,128]{2,1,0:T(8,128)} %copy-done.13, f32[40,8,128]{2,1,0:T(8,128)} %copy-done.12), custom_call_target="tpu_custom_call" | custom-call | tf_op jit(solution)/shard_map/cell_force/pallas_call | solution.py:747
  67.6 1.7 %collective-permute-start.7 = (f32[40,8,128]{2,1,0:T(8,128)}, f32[40,8,128]{2,1,0:T(8,128)S(1)}, u32[]{:S(2)}, u32[]{:S(2)}) collective-permute-start(f32[40,8,128]{2,1,0:T(8,128)} %cell_force.2.refs_0_.refs_8_), channel_id=1, source_target_pairs={{0,2},{1,3},{2,0},{3,1},{4,6},{5,7},{6,4},{7,5},{8,10},{9,11},{10,... | collective-permute-start | bytes 491528 | tf_op jit(solution)/shard_map/ppermute | solution.py:53
  69.3 0.5 collective-permute-start.11
  69.8 4.2 %collective-permute-done.7.refs_2_.refs_10_ = f32[40,8,128]{2,1,0:T(8,128)S(1)} collective-permute-done((f32[40,8,128]{2,1,0:T(8,128)}, f32[40,8,128]{2,1,0:T(8,128)S(1)}, u32[]{:S(2)}, u32[]{:S(2)}) %collective-permute-start.7) | collective-permute-done | bytes 163872 | tf_op jit(solution)/shard_map/ppermute | solution.py:53
  74.1 1.4 %collective-permute-done.8.refs_3_.refs_11_ = f32[40,8,128]{2,1,0:T(8,128)S(1)} collective-permute-done((f32[40,8,128]{2,1,0:T(8,128)S(1)}, f32[40,8,128]{2,1,0:T(8,128)S(1)}, u32[]{:S(2)}, u32[]{:S(2)}) %collective-permute-start.8) | collective-permute-done | bytes 163872 | tf_op jit(solution)/shard_map/ppermute | solution.py:57
  75.5 1.0 copy-done
  76.4 2.3 %second_moments.1 = (f32[352,128]{1,0:T(8,128)S(1)}, f32[1024,128]{1,0:T(8,128)}, f32[1024,128]{1,0:T(8,128)S(1)}) custom-call(s32[1]{0:T(128)} %bitcast.me_ref, s32[4,40]{1,0:T(4,128)S(1)} %bitcast.67, f32[1024,128]{1,0:T(8,128)S(1)} %bitcast.62, f32[1024,128]{1,0:T(8,128)S(1)} %bitcast.58, f32[1024,128]{1,0:T(8,128)S(1)} %bitcast.64, ...), custom_call_target="tpu_custom_call" | custom-call | tf_op jit(solution)/shard_map/second_moments/pallas_call | solution.py:764
  78.7 0.8 copy-done.5
  79.5 0.7 copy-done.9
  80.2 6.0 %all-to-all-start.1 = ((f32[32,1,1408]{2,1,0:T(1,128)}), f32[32,1,1408]{2,1,0:T(1,128)}, u32[]{:S(2)}, u32[]{:S(2)}) async-start(f32[32,1,1408]{2,1,0:T(1,128)} %bitcast.65), calls=%async_computation.1 | async-start | bytes 360448 | tf_op jit(solution)/shard_map/all_to_all | solution.py:652
  86.3 17.3 %near_second.1 = (f32[40,8,128]{2,1,0:T(8,128)S(1)}, f32[40,8,128]{2,1,0:T(8,128)S(1)}) custom-call(s32[1]{0:T(128)} %bitcast.me_ref, s32[4,40]{1,0:T(4,128)S(1)} %bitcast.68, s32[40,128]{1,0:T(8,128)S(1)} %copy-done.8, f32[128,8,128]{2,1,0:T(8,128)S(1)} %bitcast.59, f32[128,8,128]{2,1,0:T(8,128)S(1)} %collective-permute-done.3.refs_1_, ...), custom_call_target="tpu_custom_call" | custom-call | tf_op jit(solution)/shard_map/near_second/pallas_call | solution.py:725
  103.6 0.7 copy-done.10
  104.3 0.7 copy-done.11
  104.9 17.6 %cell_force.3.refs_0_ = f32[40,8,128]{2,1,0:T(8,128)} custom-call(s32[40,128]{1,0:T(8,128)} %copy-done.7, s32[1024]{0:T(1024)} %bitcast.82, f32[352,128]{1,0:T(8,128)} %bitcast.30.cells_ref, f32[40,8,128]{2,1,0:T(8,128)} %copy-done.11, f32[40,8,128]{2,1,0:T(8,128)} %copy-done.10), custom_call_target="tpu_custom_call" | custom-call | tf_op jit(solution)/shard_map/cell_force/pallas_call | solution.py:747
  122.5 1.5 %collective-permute-start.13 = (f32[40,8,128]{2,1,0:T(8,128)}, f32[40,8,128]{2,1,0:T(8,128)S(1)}, u32[]{:S(2)}, u32[]{:S(2)}) collective-permute-start(f32[40,8,128]{2,1,0:T(8,128)} %cell_force.3.refs_0_), channel_id=1, source_target_pairs={{0,2},{1,3},{2,0},{3,1},{4,6},{5,7},{6,4},{7,5},{8,10},{9,11},{10,... | collective-permute-start | bytes 491528 | tf_op jit(solution)/shard_map/ppermute | solution.py:53
  124.1 4.8 %collective-permute-done.13.refs_2_ = f32[40,8,128]{2,1,0:T(8,128)S(1)} collective-permute-done((f32[40,8,128]{2,1,0:T(8,128)}, f32[40,8,128]{2,1,0:T(8,128)S(1)}, u32[]{:S(2)}, u32[]{:S(2)}) %collective-permute-start.13) | collective-permute-done | bytes 163872 | tf_op jit(solution)/shard_map/ppermute | solution.py:53
  128.8 1.4 %collective-permute-done.14.refs_3_ = f32[40,8,128]{2,1,0:T(8,128)S(1)} collective-permute-done((f32[40,8,128]{2,1,0:T(8,128)S(1)}, f32[40,8,128]{2,1,0:T(8,128)S(1)}, u32[]{:S(2)}, u32[]{:S(2)}) %collective-permute-start.14) | collective-permute-done | bytes 163872 | tf_op jit(solution)/shard_map/ppermute | solution.py:57
  130.2 0.9 copy-done.4
  131.2 2.4 %final_speeds.1 = f32[1024,128]{1,0:T(8,128)} custom-call(s32[1]{0:T(128)} %bitcast.me_ref, s32[4,40]{1,0:T(4,128)S(1)} %bitcast.69, f32[1024,128]{1,0:T(8,128)S(1)} %copy-done.6, f32[40,8,128]{2,1,0:T(8,128)S(1)} %copy-done.4, f32[40,8,128]{2,1,0:T(8,128)S(1)} %collective-permute-done.12.refs_1_, f32[40,8,128]{2,1,0:T(8,128)S(1)} %collective-permute-done.13.refs_2_, ...), custom_call_target="tpu_custom_call" | custom-call | tf_op jit(solution)/shard_map/final_speeds/pallas_call | solution.py:776
  (70 shorter events, 0.6 us)
Async XLA Ops:
  0.6 0.7 copy-start.23
  2.4 1.7 %copy-start.17 = (f32[32768]{0:T(1024)S(1)}, f32[32768]{0:T(1024)}, u32[]{:S(2)}) copy-start(f32[32768]{0:T(1024)} %param.13) | copy-start | bytes 393220
  4.1 21.2 %copy-start.14 = (f32[3,32768]{1,0:T(4,128)}, f32[3,32768]{1,0:T(4,128)S(1)}, u32[]{:S(2)}) copy-start(f32[3,32768]{1,0:T(4,128)S(1)} %get-tuple-element.25) | copy-start | bytes 1179652
  4.4 1.1 copy-start.22
  4.4 1.1 copy-start.20
  5.4 0.7 copy-start.21
  6.1 0.8 copy-start.18
  6.9 0.7 copy-start.19
  7.8 3.6 %copy-start.16 = (s32[32768]{0:T(1024)S(1)}, s32[32768]{0:T(1024)}, u32[]{:S(2)}) copy-start(s32[32768]{0:T(1024)} %param.15) | copy-start | bytes 393220
  7.9 5.6 %collective-permute-start.1 = (s32[136,128]{1,0:T(8,128)S(1)}, s32[136,128]{1,0:T(8,128)S(1)}, u32[]{:S(2)}, u32[]{:S(2)}) collective-permute-start(s32[136,128]{1,0:T(8,128)S(1)} %pad.14), channel_id=1, source_target_pairs={{0,2},{1,3},{2,0},{3,1},{4,6},{5,7},{6,4},{7,5},{8,10},{9,11},{10,... | collective-permute-start | bytes 208904 | tf_op jit(solution)/shard_map/ppermute | solution.py:53
  10.9 2.6 %collective-permute-start = (s32[136,128]{1,0:T(8,128)S(1)}, s32[136,128]{1,0:T(8,128)S(1)}, u32[]{:S(2)}, u32[]{:S(2)}) collective-permute-start(s32[136,128]{1,0:T(8,128)S(1)} %pad.14), channel_id=1, source_target_pairs={{0,1},{1,0},{2,3},{3,2},{4,5},{5,4},{6,7},{7,6},{8,9},{9,8},{10,11... | collective-permute-start | bytes 208904 | tf_op jit(solution)/shard_map/ppermute | solution.py:57
  10.9 14.3 %collective-permute-start.4 = (f32[128,8,128]{2,1,0:T(8,128)S(1)}, f32[128,8,128]{2,1,0:T(8,128)S(1)}, u32[]{:S(2)}, u32[]{:S(2)}) collective-permute-start(f32[128,8,128]{2,1,0:T(8,128)S(1)} %bitcast.55), channel_id=1, source_target_pairs={{0,2},{1,3},{2,0},{3,1},{4,6},{5,7},{6,4},{7,5},{8,10},{9,11},{10,... | collective-permute-start | bytes 1572872 | tf_op jit(solution)/shard_map/ppermute | solution.py:53
  11.1 15.8 %collective-permute-start.3 = (f32[128,8,128]{2,1,0:T(8,128)S(1)}, f32[128,8,128]{2,1,0:T(8,128)S(1)}, u32[]{:S(2)}, u32[]{:S(2)}) collective-permute-start(f32[128,8,128]{2,1,0:T(8,128)S(1)} %bitcast.56), channel_id=1, source_target_pairs={{0,1},{1,0},{2,3},{3,2},{4,5},{5,4},{6,7},{7,6},{8,9},{9,8},{10,11... | collective-permute-start | bytes 1572872 | tf_op jit(solution)/shard_map/ppermute | solution.py:57
  13.5 1.3 collective-permute-start.2
  15.7 18.6 %copy-start.7 = (s32[40,128]{1,0:T(8,128)}, s32[40,128]{1,0:T(8,128)S(1)}, u32[]{:S(2)}) copy-start(s32[40,128]{1,0:T(8,128)S(1)} %select_select_fusion.list_ref) | copy-start | bytes 61444
  15.7 9.8 %copy-start.15 = (f32[32768]{0:T(1024)S(1)}, f32[32768]{0:T(1024)}, u32[]{:S(2)}) copy-start(f32[32768]{0:T(1024)} %convert_element_type.6) | copy-start | bytes 393220
  25.3 1.9 %collective-permute-start.5 = (f32[128,8,128]{2,1,0:T(8,128)S(1)}, f32[128,8,128]{2,1,0:T(8,128)S(1)}, u32[]{:S(2)}, u32[]{:S(2)}) collective-permute-start(f32[128,8,128]{2,1,0:T(8,128)S(1)} %collective-permute-done.4.refs_2_), channel_id=1, source_target_pairs={{0,1},{1,0},{2,3},{3,2},{4,5},{5,4},{6,7},{7,6},{8,9},{9,8},{10,11... | collective-permute-start | bytes 1572872 | tf_op jit(solution)/shard_map/ppermute | solution.py:57
  27.2 42.1 %collective-permute-start.10 = (f32[128,8,128]{2,1,0:T(8,128)S(1)}, f32[128,8,128]{2,1,0:T(8,128)}, u32[]{:S(2)}, u32[]{:S(2)}) collective-permute-start(f32[128,8,128]{2,1,0:T(8,128)S(1)} %bitcast.60), channel_id=1, source_target_pairs={{0,2},{1,3},{2,0},{3,1},{4,6},{5,7},{6,4},{7,5},{8,10},{9,11},{10,... | collective-permute-start | bytes 1572872 | tf_op jit(solution)/shard_map/ppermute | solution.py:53
  28.2 21.8 %all-to-all-start = ((f32[32,1,1408]{2,1,0:T(1,128)}), f32[32,1,1408]{2,1,0:T(1,128)}, u32[]{:S(2)}, u32[]{:S(2)}) async-start(f32[32,1,1408]{2,1,0:T(1,128)} %bitcast.26), calls=%async_computation | async-start | bytes 360448 | tf_op jit(solution)/shard_map/all_to_all | solution.py:652
  48.7 0.7 copy-start.12
  49.3 0.7 copy-start.13
  67.6 6.5 %collective-permute-start.7 = (f32[40,8,128]{2,1,0:T(8,128)}, f32[40,8,128]{2,1,0:T(8,128)S(1)}, u32[]{:S(2)}, u32[]{:S(2)}) collective-permute-start(f32[40,8,128]{2,1,0:T(8,128)} %cell_force.2.refs_0_.refs_8_), channel_id=1, source_target_pairs={{0,2},{1,3},{2,0},{3,1},{4,6},{5,7},{6,4},{7,5},{8,10},{9,11},{10,... | collective-permute-start | bytes 491528 | tf_op jit(solution)/shard_map/ppermute | solution.py:53
  69.3 16.9 %collective-permute-start.9 = (f32[128,8,128]{2,1,0:T(8,128)S(1)}, f32[128,8,128]{2,1,0:T(8,128)}, u32[]{:S(2)}, u32[]{:S(2)}) collective-permute-start(f32[128,8,128]{2,1,0:T(8,128)S(1)} %bitcast.61), channel_id=1, source_target_pairs={{0,1},{1,0},{2,3},{3,2},{4,5},{5,4},{6,7},{7,6},{8,9},{9,8},{10,11... | collective-permute-start | bytes 1572872 | tf_op jit(solution)/shard_map/ppermute | solution.py:57
  69.3 16.9 %collective-permute-start.11 = (f32[128,8,128]{2,1,0:T(8,128)}, f32[128,8,128]{2,1,0:T(8,128)}, u32[]{:S(2)}, u32[]{:S(2)}) collective-permute-start(f32[128,8,128]{2,1,0:T(8,128)} %collective-permute-done.10.refs_6_), channel_id=1, source_target_pairs={{0,1},{1,0},{2,3},{3,2},{4,5},{5,4},{6,7},{7,6},{8,9},{9,8},{10,11... | collective-permute-start | bytes 1572872 | tf_op jit(solution)/shard_map/ppermute | solution.py:57
  69.8 4.3 %collective-permute-start.6 = (f32[40,8,128]{2,1,0:T(8,128)}, f32[40,8,128]{2,1,0:T(8,128)S(1)}, u32[]{:S(2)}, u32[]{:S(2)}) collective-permute-start(f32[40,8,128]{2,1,0:T(8,128)} %cell_force.2.refs_0_.refs_8_), channel_id=1, source_target_pairs={{0,1},{1,0},{2,3},{3,2},{4,5},{5,4},{6,7},{7,6},{8,9},{9,8},{10,11... | collective-permute-start | bytes 491528 | tf_op jit(solution)/shard_map/ppermute | solution.py:57
  74.1 1.4 %collective-permute-start.8 = (f32[40,8,128]{2,1,0:T(8,128)S(1)}, f32[40,8,128]{2,1,0:T(8,128)S(1)}, u32[]{:S(2)}, u32[]{:S(2)}) collective-permute-start(f32[40,8,128]{2,1,0:T(8,128)S(1)} %collective-permute-done.7.refs_2_.refs_10_), channel_id=1, source_target_pairs={{0,1},{1,0},{2,3},{3,2},{4,5},{5,4},{6,7},{7,6},{8,9},{9,8},{10,11... | collective-permute-start | bytes 491528 | tf_op jit(solution)/shard_map/ppermute | solution.py:57
  75.5 3.3 %copy-start.2 = (f32[40,8,128]{2,1,0:T(8,128)}, f32[40,8,128]{2,1,0:T(8,128)S(1)}, u32[]{:S(2)}) copy-start(f32[40,8,128]{2,1,0:T(8,128)S(1)} %collective-permute-done.8.refs_3_.refs_11_) | copy-start | bytes 491524
  75.5 1.0 copy-start
  78.7 0.8 copy-start.5
  79.5 0.7 copy-start.9
  80.2 6.1 %copy-start.1 = (f32[40,8,128]{2,1,0:T(8,128)S(1)}, f32[40,8,128]{2,1,0:T(8,128)}, u32[]{:S(2)}) copy-start(f32[40,8,128]{2,1,0:T(8,128)} %cell_force.2.refs_0_.refs_8_) | copy-start | bytes 491524
  80.2 6.1 %copy-start.3 = (f32[40,8,128]{2,1,0:T(8,128)S(1)}, f32[40,8,128]{2,1,0:T(8,128)}, u32[]{:S(2)}) copy-start(f32[40,8,128]{2,1,0:T(8,128)} %copy-done.2) | copy-start | bytes 491524
  80.2 6.1 %copy-start.8 = (s32[40,128]{1,0:T(8,128)S(1)}, s32[40,128]{1,0:T(8,128)}, u32[]{:S(2)}) copy-start(s32[40,128]{1,0:T(8,128)} %copy-done.7) | copy-start | bytes 61444
  80.2 24.8 %all-to-all-start.1 = ((f32[32,1,1408]{2,1,0:T(1,128)}), f32[32,1,1408]{2,1,0:T(1,128)}, u32[]{:S(2)}, u32[]{:S(2)}) async-start(f32[32,1,1408]{2,1,0:T(1,128)} %bitcast.65), calls=%async_computation.1 | async-start | bytes 360448 | tf_op jit(solution)/shard_map/all_to_all | solution.py:652
  103.6 0.7 copy-start.10
  104.3 0.7 copy-start.11
  104.9 25.3 %copy-start.6 = (f32[1024,128]{1,0:T(8,128)S(1)}, f32[1024,128]{1,0:T(8,128)}, u32[]{:S(2)}) copy-start(f32[1024,128]{1,0:T(8,128)} %copy-done.5) | copy-start | bytes 1572868
  122.5 6.3 %collective-permute-start.13 = (f32[40,8,128]{2,1,0:T(8,128)}, f32[40,8,128]{2,1,0:T(8,128)S(1)}, u32[]{:S(2)}, u32[]{:S(2)}) collective-permute-start(f32[40,8,128]{2,1,0:T(8,128)} %cell_force.3.refs_0_), channel_id=1, source_target_pairs={{0,2},{1,3},{2,0},{3,1},{4,6},{5,7},{6,4},{7,5},{8,10},{9,11},{10,... | collective-permute-start | bytes 491528 | tf_op jit(solution)/shard_map/ppermute | solution.py:53
  124.1 4.8 %collective-permute-start.12 = (f32[40,8,128]{2,1,0:T(8,128)}, f32[40,8,128]{2,1,0:T(8,128)S(1)}, u32[]{:S(2)}, u32[]{:S(2)}) collective-permute-start(f32[40,8,128]{2,1,0:T(8,128)} %cell_force.3.refs_0_), channel_id=1, source_target_pairs={{0,1},{1,0},{2,3},{3,2},{4,5},{5,4},{6,7},{7,6},{8,9},{9,8},{10,11... | collective-permute-start | bytes 491528 | tf_op jit(solution)/shard_map/ppermute | solution.py:57
  128.8 1.4 %collective-permute-start.14 = (f32[40,8,128]{2,1,0:T(8,128)S(1)}, f32[40,8,128]{2,1,0:T(8,128)S(1)}, u32[]{:S(2)}, u32[]{:S(2)}) collective-permute-start(f32[40,8,128]{2,1,0:T(8,128)S(1)} %collective-permute-done.13.refs_2_), channel_id=1, source_target_pairs={{0,1},{1,0},{2,3},{3,2},{4,5},{5,4},{6,7},{7,6},{8,9},{9,8},{10,11... | collective-permute-start | bytes 491528 | tf_op jit(solution)/shard_map/ppermute | solution.py:57
  130.2 0.9 copy-start.4
